TPU v7x, 32 devices: a whole 2x2x4 slice. The times are simulated.
32 devices in a mesh: grp: 2 (over x), tile: 16 (over z, y, core).
Axes of the slice: x: 2, y: 2, z: 4, core: 2. Of those that a mesh axis runs over, the one named last changes fastest.
Arguments:
- site_cell: int32 [2048, 2], P(('grp', 'tile')), may hold values from 0 to 63
- site_power: float32 [2048], P(('grp', 'tile')), may hold values from -4.5 to -2
- site_tile: int32 [2048, 1], P(('grp', 'tile')), may hold values from 0 to 15; in each aligned block of 64 rows (0 to 63, 64 to 127, ...) at most 8 rows name the same one
- shadow: bfloat16 [2048, 4096], P(('grp', 'tile')), may hold values from -3.75 to 3.75
Outputs:
- count_dist: float32 [16, 8, 4096], P('tile', None, 'grp')
Inputs may be any that keep to these rules, and one draw needn't show every extreme that they name: `site_tile`: among the 64 sites of one device (aligned blocks of rows), at most 8 name the same tile; in some devices a tile is named by exactly 8.
All inputs are finite; a program needn't handle non-finite values.
Results may differ from a plain program's by a relative error of at most 0.00075.
Values may be sent and summed in bfloat16 or wider, within the bound.
No kernel may reach another device: no remote copies, remote signals or barrier semaphores. Data moves between devices by JAX's collectives and lax.ppermute only.
A program may use at most 64 MiB of HBM per device.

v0:
```python
import jax
import jax.numpy as jnp
from jax import lax
from jax.sharding import PartitionSpec as P

WIN = 64
KMAX = 8
reach_sq = 16.0


def joined(value, axis, join):
    pieces = lax.all_gather(value, axis)
    head = pieces[0]
    tail = pieces[1:]
    so_far, _ = lax.scan(lambda so_far, piece: (join(so_far, piece), None), head, tail)
    return so_far


def convolve(first_dist, second_dist, state_axis):
    count_first = first_dist.shape[state_axis]
    count_second = second_dist.shape[state_axis]
    count_out = min(count_first + count_second - 1, KMAX)
    term_list = []
    for k in range(count_out):
        running = None
        for i in range(max(0, k - count_second + 1), min(k, count_first - 1) + 1):
            product = lax.index_in_dim(
                first_dist, i, state_axis, keepdims=False
            ) * lax.index_in_dim(second_dist, k - i, state_axis, keepdims=False)
            running = product if running is None else running + product
        term_list.append(running)
    return jnp.stack(term_list, state_axis)


def merge_pair(first_dist, second_dist):
    return convolve(first_dist, second_dist, 0)


def fold_slots(slot_probs):
    detect_prob = slot_probs.astype(jnp.float32)
    states = jnp.stack([1.0 - detect_prob, detect_prob], axis=1)
    while states.shape[0] > 1:
        if states.shape[0] % 2:
            count_states = states.shape[1]
            columns = states.shape[2]
            identity = jnp.concatenate(
                [
                    jnp.ones((1, 1, columns), jnp.float32),
                    jnp.zeros((1, count_states - 1, columns), jnp.float32),
                ],
                axis=1,
            )
            states = jnp.concatenate([states, identity], axis=0)
        states = convolve(states[0::2], states[1::2], 1)
    result = states[0]
    if result.shape[0] < KMAX:
        result = jnp.concatenate(
            [result, jnp.zeros((KMAX - result.shape[0], result.shape[1]), jnp.float32)], axis=0
        )
    return result


def fold_columns(slot_probs, block_width):
    slots, columns = slot_probs.shape
    blocks = slot_probs.reshape(slots, columns // block_width, block_width).transpose(1, 0, 2)
    folded = lax.map(fold_slots, blocks)
    return folded.transpose(1, 0, 2).reshape(KMAX, columns)


def site_probs(site_cell, site_power, shadow):
    cell_index = jnp.arange(shadow.shape[1], dtype=jnp.int32)
    cell_row = (cell_index // WIN).astype(jnp.float32)
    cell_col = (cell_index % WIN).astype(jnp.float32)
    row_gap = cell_row[None, :] - site_cell[:, 0:1].astype(jnp.float32)
    col_gap = cell_col[None, :] - site_cell[:, 1:2].astype(jnp.float32)
    margin = (
        site_power[:, None]
        - jnp.log(1.0 + (row_gap * row_gap + col_gap * col_gap) / reach_sq)
        + shadow.astype(jnp.float32)
    )
    return jax.nn.sigmoid(margin).astype(jnp.bfloat16)


def on_device(site_cell, site_power, site_tile, shadow):
    tiles = lax.axis_size("tile")
    groups = lax.axis_size("grp")
    site_count = shadow.shape[0]
    capacity = max(2, 2 * site_count // tiles)
    cells_all = shadow.shape[1]
    width = cells_all // groups
    detect_prob = site_probs(site_cell, site_power, shadow)
    owner_tile = site_tile[:, 0]
    hit_table = (owner_tile[:, None] == jnp.arange(tiles, dtype=jnp.int32)[None, :]).astype(
        jnp.int32
    )
    slot_rank = jnp.sum((jnp.cumsum(hit_table, axis=0) - hit_table) * hit_table, axis=1)
    slot_index = owner_tile * capacity + slot_rank
    selector = (
        slot_index[None, :] == jnp.arange(tiles * capacity, dtype=jnp.int32)[:, None]
    ).astype(jnp.bfloat16)
    outgoing = jnp.dot(selector, detect_prob, preferred_element_type=jnp.float32).astype(
        jnp.bfloat16
    )
    outgoing = outgoing.reshape(tiles * capacity, groups, width)
    items = jnp.moveaxis(
        lax.all_to_all(outgoing, "tile", split_axis=0, concat_axis=0, tiled=True), 1, 0
    )
    folded = lax.map(lambda piece: fold_columns(piece, min(piece.shape[1], 512)), items)
    group_dist = jnp.moveaxis(folded, 0, 1)
    merged = joined(group_dist, "grp", merge_pair)
    own_states = lax.dynamic_index_in_dim(merged, lax.axis_index("grp"), 1, keepdims=False)
    return own_states[None, :, :]


def solution(mesh):
    placed = (
        P(("grp", "tile"), None),
        P(("grp", "tile")),
        P(("grp", "tile"), None),
        P(("grp", "tile"), None),
    )
    return jax.shard_map(
        on_device, mesh=mesh, in_specs=placed, out_specs=P("tile", None, "grp"), check_vma=False
    )
```

profile of v0, /device:TPU:11, one launch (start us, length us, event | category | flops | bytes accessed | tf_op | source)
XLA Modules:
  0.0 92.0 jit_solution(106595305176104086)
XLA Ops:
  0.0 0.7 fusion.24
  0.8 0.8 select_reduce_fusion
  1.7 0.7 multiply_add_fusion.35
  2.3 0.8 convert_bitcast_fusion.1
  3.1 2.0 %convolution_convert_fusion = bf16[128,4096]{1,0:T(8,128)(2,1)S(1)} fusion(bf16[64,4096]{1,0:T(8,128)(2,1)} %param.11, f32[64]{0:T(128)S(1)} %get-tuple-element.135, f32[4096]{0:T(1024)S(1)} %get-tuple-element.137, f32[64]{0:T(128)S(1)} %get-tuple-element.134, f32[4096]{0:T(1024)S(1)} %get-tuple-element.136, f32[64]{0:T(128)} %param.9, ...), kind=kOutput, calls=%fused_computation.71 | convolution fusion | flops 71311360 | bytes 1606656 | tf_op jit(solution)/shard_map/dot_general | solution.py:101
  5.1 1.6 %reshape.1052 = bf16[128,2,2048]{2,1,0:T(2,128)(2,1)} reshape(bf16[128,4096]{1,0:T(8,128)(2,1)S(1)} %convolution_convert_fusion) | data formatting | bytes 2097152 | tf_op jit(solution)/shard_map/reshape | solution.py:104
  6.7 6.6 %all-to-all-start = ((bf16[128,2,2048]{2,1,0:T(2,128)(2,1)}), bf16[128,2,2048]{2,1,0:T(2,128)(2,1)S(1)}, u32[]{:S(2)}, u32[]{:S(2)}) async-start(bf16[128,2,2048]{2,1,0:T(2,128)(2,1)} %reshape.1052), calls=%async_computation | async-start | bytes 2097152 | tf_op jit(solution)/shard_map/all_to_all | solution.py:106
  13.3 24.8 %all-to-all-done = bf16[128,2,2048]{2,1,0:T(2,128)(2,1)S(1)} async-done(((bf16[128,2,2048]{2,1,0:T(2,128)(2,1)}), bf16[128,2,2048]{2,1,0:T(2,128)(2,1)S(1)}, u32[]{:S(2)}, u32[]{:S(2)}) %all-to-all-start) | async-done | bytes 1048608 | tf_op jit(solution)/shard_map/all_to_all | solution.py:106
  38.5 45.9 %while.25 = (s32[]{:T(128)}, f32[2,8,2048]{2,1,0:T(8,128)S(1)}, bf16[2,128,2048]{2,1,0:T(8,128)(2,1)S(1)}, s32[]{:T(128)}, s32[]{:T(128)}, /*index=5*/s32[]{:T(128)}) while((s32[]{:T(128)}, f32[2,8,2048]{2,1,0:T(8,128)S(1)}, bf16[2,128,2048]{2,1,0:T(8,128)(2,1)S(1)}, s32[]{:T(128)}, s32[]{:T(128)}, /*index=5*/s32[]{:T(128)}) %tuple.136), condition=%wide.region_5.6_spmd, body=%wide.region_2.5_spmd.sunk | while | flops 1654788 | bytes 14295218 | solution.py:108
  39.0 22.5 %while.26 = (s32[]{:T(128)}, f32[4,8,512]{2,1,0:T(8,128)S(1)}, bf16[4,128,512]{2,0,1:T(4,128)(2,1)S(1)}, s32[]{:T(128)}) while((s32[]{:T(128)}, f32[4,8,512]{2,1,0:T(8,128)S(1)}, bf16[4,128,512]{2,0,1:T(4,128)(2,1)S(1)}, s32[]{:T(128)}) %tuple.139), condition=%wide.region_4.4_spmd, body=%wide.region_3.3_spmd.sunk | while | flops 1654786 | bytes 12066877 | solution.py:66
  39.4 0.5 pad_maximum_fusion.4
  41.1 0.5 stack.31
  42.4 0.4 stack.32
  45.0 0.5 pad_maximum_fusion.4
  46.7 0.5 stack.31
  48.0 0.4 stack.32
  50.6 0.5 pad_maximum_fusion.4
  52.3 0.5 stack.31
  53.6 0.4 stack.32
  56.2 0.5 pad_maximum_fusion.4
  57.9 0.5 stack.31
  61.9 22.5 %while.26 = (s32[]{:T(128)}, f32[4,8,512]{2,1,0:T(8,128)S(1)}, bf16[4,128,512]{2,0,1:T(4,128)(2,1)S(1)}, s32[]{:T(128)}) while((s32[]{:T(128)}, f32[4,8,512]{2,1,0:T(8,128)S(1)}, bf16[4,128,512]{2,0,1:T(4,128)(2,1)S(1)}, s32[]{:T(128)}) %tuple.139), condition=%wide.region_4.4_spmd, body=%wide.region_3.3_spmd.sunk | while | flops 1654786 | bytes 12066877 | solution.py:66
  62.3 0.5 pad_maximum_fusion.4
  64.0 0.5 stack.31
  67.9 0.5 pad_maximum_fusion.4
  69.6 0.5 stack.31
  73.6 0.5 pad_maximum_fusion.4
  75.2 0.5 stack.31
  79.2 0.5 pad_maximum_fusion.4
  80.9 0.5 stack.31
  84.4 6.0 %all-gather = f32[16,2,2048]{2,0,1:T(8,128)S(1)} all-gather(f32[8,2,2048]{2,0,1:T(8,128)S(1)} %bitcast.234), channel_id=2, replica_groups=mesh['grp'=2,'tile'=16] {'grp'}, dimensions={0}, use_global_device_ids=true | all-gather | bytes 393216 | tf_op jit(solution)/shard_map/all_gather | solution.py:12
  91.3 0.6 dynamic-slice_bitcast_fusion
  (286 shorter events, 35.7 us)
Async XLA Ops:
  6.7 31.5 %all-to-all-start = ((bf16[128,2,2048]{2,1,0:T(2,128)(2,1)}), bf16[128,2,2048]{2,1,0:T(2,128)(2,1)S(1)}, u32[]{:S(2)}, u32[]{:S(2)}) async-start(bf16[128,2,2048]{2,1,0:T(2,128)(2,1)} %reshape.1052), calls=%async_computation | async-start | bytes 2097152 | tf_op jit(solution)/shard_map/all_to_all | solution.py:106
where the time goes:
time: 92.2 us; the launch traced here: 92 us
  other arithmetic  34.7 us (38%)
  waiting for transfers between devices  24.8 us (27%)
  local copies, waits for them, and re-layouts  15.6 us (17%)
  starting transfers between devices  6.61 us (7%)
  blocking collectives  5.99 us (6%)
  loops' own time  2.16 us (2%)
  matrix products  2.01 us (2%)
    all_to_all x1, waiting for transfers between devices, on_device(): lax.all_to_all(outgoing, 'tile', split_axis=0, concat_axis=0, tiled=True)  24.8 us
    add x156, other arithmetic, convolve(): running = product if running is None else running + product  16.5 us
    another operation x41, local copies, waits for them, and re-layouts, convolve(): return jnp.stack(term_list, state_axis)  10.5 us
    all_to_all x1, starting transfers between devices, on_device(): lax.all_to_all(outgoing, 'tile', split_axis=0, concat_axis=0, tiled=True)  6.61 us
    all_gather x1, blocking collectives, joined(): pieces = lax.all_gather(value, axis)  5.99 us
    mul x16, other arithmetic, convolve(): lax.index_in_dim(first_dist, i, state_axis, keepdims=False)  5.62 us
    another operation x8, other arithmetic, fold_slots(): states = jnp.stack([1.0 - detect_prob, detect_prob], axis=1)  3.81 us
    sub x8, other arithmetic, fold_slots(): states = jnp.stack([1.0 - detect_prob, detect_prob], axis=1)  2.91 us
  transfers between devices with their start and end apart: 1, of which 1 were waited for; matrix products, arithmetic and copies ran while one was open for 0% of the time, Pallas kernels for 0%

commit v1 on v0

--- a/solution.py
+++ b/solution.py
@@ -6,6 +6,22 @@
 WIN = 64
 KMAX = 8
 reach_sq = 16.0
+
+
+def exchange_in_pairs(x, axis, split, join):
+    ways, here = (lax.axis_size(axis), lax.axis_index(axis))
+    width = x.shape[split] // ways
+    dims = list(x.shape)
+    dims[split] = width
+    height = dims[join]
+    dims[join] = height * ways
+    full = jnp.zeros(dims, x.dtype)
+    for mask in range(ways):
+        part = lax.dynamic_slice_in_dim(x, (here ^ mask) * width, width, axis=split)
+        if mask:
+            part = lax.ppermute(part, axis, [(d, d ^ mask) for d in range(ways)])
+        full = lax.dynamic_update_slice_in_dim(full, part, (here ^ mask) * height, axis=join)
+    return full
 
 
 def joined(value, axis, join):
@@ -102,9 +118,7 @@
         jnp.bfloat16
     )
     outgoing = outgoing.reshape(tiles * capacity, groups, width)
-    items = jnp.moveaxis(
-        lax.all_to_all(outgoing, "tile", split_axis=0, concat_axis=0, tiled=True), 1, 0
-    )
+    items = jnp.moveaxis(exchange_in_pairs(outgoing, "tile", 0, 0), 1, 0)
     folded = lax.map(lambda piece: fold_columns(piece, min(piece.shape[1], 512)), items)
     group_dist = jnp.moveaxis(folded, 0, 1)
     merged = joined(group_dist, "grp", merge_pair)

time: 92.2 us -> 95.6 us (1.037)
  starting transfers between devices: 6.61 us -> 19.2 us
  waiting for transfers between devices: 24.8 us -> 14.7 us
    all_to_all x1 -> x0, waiting for transfers between devices: 24.8 us -> none  [on_device(): lax.all_to_all(outgoing, 'tile', split_axis=0, concat_axis=0, tiled=True)]
    ppermute x0 -> x15, starting transfers between devices: none -> 19.2 us  [exchange_in_pairs(): part = lax.ppermute(part, axis, [(d, d ^ mask) for d in range(ways)])]
    ppermute x0 -> x15, waiting for transfers between devices: none -> 14.7 us  [exchange_in_pairs(): part = lax.ppermute(part, axis, [(d, d ^ mask) for d in range(ways)])]
    all_to_all x1 -> x0, starting transfers between devices: 6.61 us -> none  [on_device(): lax.all_to_all(outgoing, 'tile', split_axis=0, concat_axis=0, tiled=True)]
    dynamic_slice x0 -> x1, local copies, waits for them, and re-layouts: none -> 1.1 us  [exchange_in_pairs(): part = lax.dynamic_slice_in_dim(x, (here ^ mask) * width, width, axis=split)]
  transfers between devices with their start and end apart: 1 -> 15, of which waited for: 1 -> 6; matrix products, arithmetic and copies ran while one was open for 0% -> 1% of each run, Pallas kernels for 0% -> 0%
where the time goes in v1:
time: 95.6 us; the launch traced here: 94.7 us
  other arithmetic  34.7 us (36%)
  starting transfers between devices  19.2 us (20%)
  local copies, waits for them, and re-layouts  16.2 us (17%)
  waiting for transfers between devices  14.7 us (15%)
  blocking collectives  5.36 us (6%)
  loops' own time  2.16 us (2%)
  matrix products  2.01 us (2%)
    ppermute x15, starting transfers between devices, exchange_in_pairs(): part = lax.ppermute(part, axis, [(d, d ^ mask) for d in range(ways)])  19.2 us
    add x156, other arithmetic, convolve(): running = product if running is None else running + product  16.5 us
    ppermute x15, waiting for transfers between devices, exchange_in_pairs(): part = lax.ppermute(part, axis, [(d, d ^ mask) for d in range(ways)])  14.7 us
    another operation x41, local copies, waits for them, and re-layouts, convolve(): return jnp.stack(term_list, state_axis)  10.5 us
    mul x16, other arithmetic, convolve(): lax.index_in_dim(first_dist, i, state_axis, keepdims=False)  5.62 us
    all_gather x1, blocking collectives, joined(): pieces = lax.all_gather(value, axis)  5.36 us
    another operation x8, other arithmetic, fold_slots(): states = jnp.stack([1.0 - detect_prob, detect_prob], axis=1)  3.81 us
    sub x8, other arithmetic, fold_slots(): states = jnp.stack([1.0 - detect_prob, detect_prob], axis=1)  2.91 us
  transfers between devices with their start and end apart: 15, of which 6 were waited for; matrix products, arithmetic and copies ran while one was open for 1% of the time, Pallas kernels for 0%

profile of v1, /device:TPU:11, one launch (start us, length us, event | category | flops | bytes accessed | tf_op | source)
XLA Modules:
  0.0 94.7 jit_solution(6734185073316448563)
XLA Ops:
  0.0 0.7 fusion.24
  0.8 0.8 select_reduce_fusion
  1.7 0.7 multiply_add_fusion.35
  2.3 0.8 convert_bitcast_fusion.1
  3.1 2.0 %convolution_convert_fusion = bf16[128,4096]{1,0:T(8,128)(2,1)S(1)} fusion(bf16[64,4096]{1,0:T(8,128)(2,1)} %param.11, f32[64]{0:T(128)S(1)} %get-tuple-element.148, f32[4096]{0:T(1024)S(1)} %get-tuple-element.150, f32[64]{0:T(128)S(1)} %get-tuple-element.147, f32[4096]{0:T(1024)S(1)} %get-tuple-element.149, f32[64]{0:T(128)} %param.9, ...), kind=kOutput, calls=%fused_computation.71 | convolution fusion | flops 71311360 | bytes 1606656 | tf_op jit(solution)/shard_map/dot_general | solution.py:117
  5.1 0.8 reshape.1052
  6.0 1.1 %constant_dynamic-slice_fusion.1 = (bf16[8,2,2048]{2,1,0:T(2,128)(2,1)S(1)}, bf16[8,2,2048]{2,1,0:T(2,128)(2,1)S(1)}, bf16[8,2,2048]{2,1,0:T(2,128)(2,1)S(1)}, b...) fusion(bf16[128,2,2048]{2,1,0:T(2,128)(2,1)S(1)} %reshape.1052,, ...), kind=kLoop, calls=%fused_computation.130 | loop fusion | bytes 2097216 | tf_op jit(solution)/shard_map/dynamic_slice | solution.py:20
  7.1 0.7 collective-permute-start
  7.9 1.3 %collective-permute-start.1 = (bf16[8,2,2048]{2,0,1:T(8,128)(2,1)S(1)}, bf16[8,2,2048]{2,0,1:T(8,128)(2,1)S(1)}, u32[]{:S(2)}, u32[]{:S(2)}) collective-permute-start(bf16[8,2,2048]{2,0,1:T(8,128)(2,1)S(1)} %copy.39), channel_id=1, source_target_pairs={{0,2},{1,3},{2,0},{3,1},{4,6},{5,7},{6,4},{7,5},{8,10},{9,11},{10,... | collective-permute-start | bytes 196616 | tf_op jit(solution)/shard_map/ppermute | solution.py:22
  10.0 1.7 %collective-permute-start.4 = (bf16[8,2,2048]{2,0,1:T(8,128)(2,1)S(1)}, bf16[8,2,2048]{2,0,1:T(8,128)(2,1)S(1)}, u32[]{:S(2)}, u32[]{:S(2)}) collective-permute-start(bf16[8,2,2048]{2,0,1:T(8,128)(2,1)S(1)} %copy.42), channel_id=1, source_target_pairs={{0,5},{1,4},{2,7},{3,6},{4,1},{5,0},{6,3},{7,2},{8,13},{9,12},{10,... | collective-permute-start | bytes 196616 | tf_op jit(solution)/shard_map/ppermute | solution.py:22
  12.2 1.2 %collective-permute-start.5 = (bf16[8,2,2048]{2,0,1:T(8,128)(2,1)S(1)}, bf16[8,2,2048]{2,0,1:T(8,128)(2,1)S(1)}, u32[]{:S(2)}, u32[]{:S(2)}) collective-permute-start(bf16[8,2,2048]{2,0,1:T(8,128)(2,1)S(1)} %copy.43), channel_id=1, source_target_pairs={{0,6},{1,7},{2,4},{3,5},{4,2},{5,3},{6,0},{7,1},{8,14},{9,15},{10,... | collective-permute-start | bytes 196616 | tf_op jit(solution)/shard_map/ppermute | solution.py:22
  13.5 1.5 %collective-permute-start.6 = (bf16[8,2,2048]{2,0,1:T(8,128)(2,1)S(1)}, bf16[8,2,2048]{2,0,1:T(8,128)(2,1)S(1)}, u32[]{:S(2)}, u32[]{:S(2)}) collective-permute-start(bf16[8,2,2048]{2,0,1:T(8,128)(2,1)S(1)} %copy.44), channel_id=1, source_target_pairs={{0,7},{1,6},{2,5},{3,4},{4,3},{5,2},{6,1},{7,0},{8,15},{9,14},{10,... | collective-permute-start | bytes 196616 | tf_op jit(solution)/shard_map/ppermute | solution.py:22
  15.0 2.4 %collective-permute-start.7 = (bf16[8,2,2048]{2,0,1:T(8,128)(2,1)S(1)}, bf16[8,2,2048]{2,0,1:T(8,128)(2,1)S(1)}, u32[]{:S(2)}, u32[]{:S(2)}) collective-permute-start(bf16[8,2,2048]{2,0,1:T(8,128)(2,1)S(1)} %copy.45), channel_id=1, source_target_pairs={{0,8},{1,9},{2,10},{3,11},{4,12},{5,13},{6,14},{7,15},{8,0},{9,1},... | collective-permute-start | bytes 196616 | tf_op jit(solution)/shard_map/ppermute | solution.py:22
  17.9 3.3 %collective-permute-start.9 = (bf16[8,2,2048]{2,0,1:T(8,128)(2,1)S(1)}, bf16[8,2,2048]{2,0,1:T(8,128)(2,1)S(1)}, u32[]{:S(2)}, u32[]{:S(2)}) collective-permute-start(bf16[8,2,2048]{2,0,1:T(8,128)(2,1)S(1)} %copy.47), channel_id=1, source_target_pairs={{0,10},{1,11},{2,8},{3,9},{4,14},{5,15},{6,12},{7,13},{8,2},{9,3},... | collective-permute-start | bytes 196616 | tf_op jit(solution)/shard_map/ppermute | solution.py:22
  21.6 1.4 %collective-permute-start.11 = (bf16[8,2,2048]{2,0,1:T(8,128)(2,1)S(1)}, bf16[8,2,2048]{2,0,1:T(8,128)(2,1)S(1)}, u32[]{:S(2)}, u32[]{:S(2)}) collective-permute-start(bf16[8,2,2048]{2,0,1:T(8,128)(2,1)S(1)} %copy.49), channel_id=1, source_target_pairs={{0,12},{1,13},{2,14},{3,15},{4,8},{5,9},{6,10},{7,11},{8,4},{9,5},... | collective-permute-start | bytes 196616 | tf_op jit(solution)/shard_map/ppermute | solution.py:22
  23.0 0.6 collective-permute-start.12
  23.5 3.9 %collective-permute-done.8 = bf16[8,2,2048]{2,0,1:T(8,128)(2,1)S(1)} collective-permute-done((bf16[8,2,2048]{2,0,1:T(8,128)(2,1)S(1)}, bf16[8,2,2048]{2,0,1:T(8,128)(2,1)S(1)}, u32[]{:S(2)}, u32[]{:S(2)}) %collective-permute-start.8) | collective-permute-done | bytes 65568 | tf_op jit(solution)/shard_map/ppermute | solution.py:22
  27.4 0.9 %collective-permute-start.13 = (bf16[8,2,2048]{2,0,1:T(8,128)(2,1)S(1)}, bf16[8,2,2048]{2,0,1:T(8,128)(2,1)S(1)}, u32[]{:S(2)}, u32[]{:S(2)}) collective-permute-start(bf16[8,2,2048]{2,0,1:T(8,128)(2,1)S(1)} %copy.51), channel_id=1, source_target_pairs={{0,14},{1,15},{2,12},{3,13},{4,10},{5,11},{6,8},{7,9},{8,6},{9,7},... | collective-permute-start | bytes 196616 | tf_op jit(solution)/shard_map/ppermute | solution.py:22
  28.4 0.6 collective-permute-done.9
  29.0 2.7 %collective-permute-start.14 = (bf16[8,2,2048]{2,0,1:T(8,128)(2,1)S(1)}, bf16[8,2,2048]{2,0,1:T(8,128)(2,1)S(1)}, u32[]{:S(2)}, u32[]{:S(2)}) collective-permute-start(bf16[8,2,2048]{2,0,1:T(8,128)(2,1)S(1)} %copy.52), channel_id=1, source_target_pairs={{0,15},{1,14},{2,13},{3,12},{4,11},{5,10},{6,9},{7,8},{8,7},{9,6},... | collective-permute-start | bytes 196616 | tf_op jit(solution)/shard_map/ppermute | solution.py:22
  31.7 2.9 %collective-permute-done.11 = bf16[8,2,2048]{2,0,1:T(8,128)(2,1)S(1)} collective-permute-done((bf16[8,2,2048]{2,0,1:T(8,128)(2,1)S(1)}, bf16[8,2,2048]{2,0,1:T(8,128)(2,1)S(1)}, u32[]{:S(2)}, u32[]{:S(2)}) %collective-permute-start.11) | collective-permute-done | bytes 65568 | tf_op jit(solution)/shard_map/ppermute | solution.py:22
  34.6 2.8 %collective-permute-done.12 = bf16[8,2,2048]{2,0,1:T(8,128)(2,1)S(1)} collective-permute-done((bf16[8,2,2048]{2,0,1:T(8,128)(2,1)S(1)}, bf16[8,2,2048]{2,0,1:T(8,128)(2,1)S(1)}, u32[]{:S(2)}, u32[]{:S(2)}) %collective-permute-start.12) | collective-permute-done | bytes 65568 | tf_op jit(solution)/shard_map/ppermute | solution.py:22
  37.4 3.1 %collective-permute-done.13 = bf16[8,2,2048]{2,0,1:T(8,128)(2,1)S(1)} collective-permute-done((bf16[8,2,2048]{2,0,1:T(8,128)(2,1)S(1)}, bf16[8,2,2048]{2,0,1:T(8,128)(2,1)S(1)}, u32[]{:S(2)}, u32[]{:S(2)}) %collective-permute-start.13) | collective-permute-done | bytes 65568 | tf_op jit(solution)/shard_map/ppermute | solution.py:22
  40.5 1.4 %collective-permute-done.14 = bf16[8,2,2048]{2,0,1:T(8,128)(2,1)S(1)} collective-permute-done((bf16[8,2,2048]{2,0,1:T(8,128)(2,1)S(1)}, bf16[8,2,2048]{2,0,1:T(8,128)(2,1)S(1)}, u32[]{:S(2)}, u32[]{:S(2)}) %collective-permute-start.14) | collective-permute-done | bytes 65568 | tf_op jit(solution)/shard_map/ppermute | solution.py:22
  41.9 45.9 %while.25 = (s32[]{:T(128)}, f32[2,8,2048]{2,1,0:T(8,128)S(1)}, bf16[2,128,2048]{2,1,0:T(8,128)(2,1)S(1)}, s32[]{:T(128)}, s32[]{:T(128)}, /*index=5*/s32[]{:T(128)}) while((s32[]{:T(128)}, f32[2,8,2048]{2,1,0:T(8,128)S(1)}, bf16[2,128,2048]{2,1,0:T(8,128)(2,1)S(1)}, s32[]{:T(128)}, s32[]{:T(128)}, /*index=5*/s32[]{:T(128)}) %tuple.154), condition=%wide.region_5.6_spmd, body=%wide.region_2.5_spmd.sunk | while | flops 1654788 | bytes 14295218 | solution.py:122
  42.4 22.5 %while.26 = (s32[]{:T(128)}, f32[4,8,512]{2,1,0:T(8,128)S(1)}, bf16[4,128,512]{2,0,1:T(4,128)(2,1)S(1)}, s32[]{:T(128)}) while((s32[]{:T(128)}, f32[4,8,512]{2,1,0:T(8,128)S(1)}, bf16[4,128,512]{2,0,1:T(4,128)(2,1)S(1)}, s32[]{:T(128)}) %tuple.153), condition=%wide.region_4.4_spmd, body=%wide.region_3.3_spmd.sunk | while | flops 1654786 | bytes 12066877 | solution.py:82
  61.3 0.5 stack.31
  65.3 22.5 %while.26 = (s32[]{:T(128)}, f32[4,8,512]{2,1,0:T(8,128)S(1)}, bf16[4,128,512]{2,0,1:T(4,128)(2,1)S(1)}, s32[]{:T(128)}) while((s32[]{:T(128)}, f32[4,8,512]{2,1,0:T(8,128)S(1)}, bf16[4,128,512]{2,0,1:T(4,128)(2,1)S(1)}, s32[]{:T(128)}) %tuple.153), condition=%wide.region_4.4_spmd, body=%wide.region_3.3_spmd.sunk | while | flops 1654786 | bytes 12066877 | solution.py:82
  67.4 0.5 stack.31
  73.0 0.5 stack.31
  87.8 5.4 %all-gather = f32[16,2,2048]{2,0,1:T(8,128)S(1)} all-gather(f32[8,2,2048]{2,0,1:T(8,128)S(1)} %bitcast.234), channel_id=2, replica_groups=mesh['grp'=2,'tile'=16] {'grp'}, dimensions={0}, use_global_device_ids=true | all-gather | bytes 393216 | tf_op jit(solution)/shard_map/all_gather | solution.py:28
  94.1 0.6 dynamic-slice_bitcast_fusion
  (346 shorter events, 45.2 us)
Async XLA Ops:
  7.1 5.1 %collective-permute-start = (bf16[8,2,2048]{2,0,1:T(8,128)(2,1)S(1)}, bf16[8,2,2048]{2,0,1:T(8,128)(2,1)S(1)}, u32[]{:S(2)}, u32[]{:S(2)}) collective-permute-start(bf16[8,2,2048]{2,0,1:T(8,128)(2,1)S(1)} %copy.38), channel_id=1, source_target_pairs={{0,1},{1,0},{2,3},{3,2},{4,5},{5,4},{6,7},{7,6},{8,9},{9,8},{10,11... | collective-permute-start | bytes 196616 | tf_op jit(solution)/shard_map/ppermute | solution.py:22
  7.9 5.5 %collective-permute-start.1 = (bf16[8,2,2048]{2,0,1:T(8,128)(2,1)S(1)}, bf16[8,2,2048]{2,0,1:T(8,128)(2,1)S(1)}, u32[]{:S(2)}, u32[]{:S(2)}) collective-permute-start(bf16[8,2,2048]{2,0,1:T(8,128)(2,1)S(1)} %copy.39), channel_id=1, source_target_pairs={{0,2},{1,3},{2,0},{3,1},{4,6},{5,7},{6,4},{7,5},{8,10},{9,11},{10,... | collective-permute-start | bytes 196616 | tf_op jit(solution)/shard_map/ppermute | solution.py:22
  9.2 5.7 %collective-permute-start.2 = (bf16[8,2,2048]{2,0,1:T(8,128)(2,1)S(1)}, bf16[8,2,2048]{2,0,1:T(8,128)(2,1)S(1)}, u32[]{:S(2)}, u32[]{:S(2)}) collective-permute-start(bf16[8,2,2048]{2,0,1:T(8,128)(2,1)S(1)} %copy.40), channel_id=1, source_target_pairs={{0,3},{1,2},{2,1},{3,0},{4,7},{5,6},{6,5},{7,4},{8,11},{9,10},{10,... | collective-permute-start | bytes 196616 | tf_op jit(solution)/shard_map/ppermute | solution.py:22
  9.7 7.6 %collective-permute-start.3 = (bf16[8,2,2048]{2,0,1:T(8,128)(2,1)S(1)}, bf16[8,2,2048]{2,0,1:T(8,128)(2,1)S(1)}, u32[]{:S(2)}, u32[]{:S(2)}) collective-permute-start(bf16[8,2,2048]{2,0,1:T(8,128)(2,1)S(1)} %copy.41), channel_id=1, source_target_pairs={{0,4},{1,5},{2,6},{3,7},{4,0},{5,1},{6,2},{7,3},{8,12},{9,13},{10,... | collective-permute-start | bytes 196616 | tf_op jit(solution)/shard_map/ppermute | solution.py:22
  10.0 7.9 %collective-permute-start.4 = (bf16[8,2,2048]{2,0,1:T(8,128)(2,1)S(1)}, bf16[8,2,2048]{2,0,1:T(8,128)(2,1)S(1)}, u32[]{:S(2)}, u32[]{:S(2)}) collective-permute-start(bf16[8,2,2048]{2,0,1:T(8,128)(2,1)S(1)} %copy.42), channel_id=1, source_target_pairs={{0,5},{1,4},{2,7},{3,6},{4,1},{5,0},{6,3},{7,2},{8,13},{9,12},{10,... | collective-permute-start | bytes 196616 | tf_op jit(solution)/shard_map/ppermute | solution.py:22
  12.2 9.0 %collective-permute-start.5 = (bf16[8,2,2048]{2,0,1:T(8,128)(2,1)S(1)}, bf16[8,2,2048]{2,0,1:T(8,128)(2,1)S(1)}, u32[]{:S(2)}, u32[]{:S(2)}) collective-permute-start(bf16[8,2,2048]{2,0,1:T(8,128)(2,1)S(1)} %copy.43), channel_id=1, source_target_pairs={{0,6},{1,7},{2,4},{3,5},{4,2},{5,3},{6,0},{7,1},{8,14},{9,15},{10,... | collective-permute-start | bytes 196616 | tf_op jit(solution)/shard_map/ppermute | solution.py:22
  13.5 8.1 %collective-permute-start.6 = (bf16[8,2,2048]{2,0,1:T(8,128)(2,1)S(1)}, bf16[8,2,2048]{2,0,1:T(8,128)(2,1)S(1)}, u32[]{:S(2)}, u32[]{:S(2)}) collective-permute-start(bf16[8,2,2048]{2,0,1:T(8,128)(2,1)S(1)} %copy.44), channel_id=1, source_target_pairs={{0,7},{1,6},{2,5},{3,4},{4,3},{5,2},{6,1},{7,0},{8,15},{9,14},{10,... | collective-permute-start | bytes 196616 | tf_op jit(solution)/shard_map/ppermute | solution.py:22
  15.0 8.0 %collective-permute-start.7 = (bf16[8,2,2048]{2,0,1:T(8,128)(2,1)S(1)}, bf16[8,2,2048]{2,0,1:T(8,128)(2,1)S(1)}, u32[]{:S(2)}, u32[]{:S(2)}) collective-permute-start(bf16[8,2,2048]{2,0,1:T(8,128)(2,1)S(1)} %copy.45), channel_id=1, source_target_pairs={{0,8},{1,9},{2,10},{3,11},{4,12},{5,13},{6,14},{7,15},{8,0},{9,1},... | collective-permute-start | bytes 196616 | tf_op jit(solution)/shard_map/ppermute | solution.py:22
  17.4 10.1 %collective-permute-start.8 = (bf16[8,2,2048]{2,0,1:T(8,128)(2,1)S(1)}, bf16[8,2,2048]{2,0,1:T(8,128)(2,1)S(1)}, u32[]{:S(2)}, u32[]{:S(2)}) collective-permute-start(bf16[8,2,2048]{2,0,1:T(8,128)(2,1)S(1)} %copy.46), channel_id=1, source_target_pairs={{0,9},{1,8},{2,11},{3,10},{4,13},{5,12},{6,15},{7,14},{8,1},{9,0},... | collective-permute-start | bytes 196616 | tf_op jit(solution)/shard_map/ppermute | solution.py:22
  17.9 11.1 %collective-permute-start.9 = (bf16[8,2,2048]{2,0,1:T(8,128)(2,1)S(1)}, bf16[8,2,2048]{2,0,1:T(8,128)(2,1)S(1)}, u32[]{:S(2)}, u32[]{:S(2)}) collective-permute-start(bf16[8,2,2048]{2,0,1:T(8,128)(2,1)S(1)} %copy.47), channel_id=1, source_target_pairs={{0,10},{1,11},{2,8},{3,9},{4,14},{5,15},{6,12},{7,13},{8,2},{9,3},... | collective-permute-start | bytes 196616 | tf_op jit(solution)/shard_map/ppermute | solution.py:22
  21.2 10.5 %collective-permute-start.10 = (bf16[8,2,2048]{2,0,1:T(8,128)(2,1)S(1)}, bf16[8,2,2048]{2,0,1:T(8,128)(2,1)S(1)}, u32[]{:S(2)}, u32[]{:S(2)}) collective-permute-start(bf16[8,2,2048]{2,0,1:T(8,128)(2,1)S(1)} %copy.48), channel_id=1, source_target_pairs={{0,11},{1,10},{2,9},{3,8},{4,15},{5,14},{6,13},{7,12},{8,3},{9,2},... | collective-permute-start | bytes 196616 | tf_op jit(solution)/shard_map/ppermute | solution.py:22
  21.6 13.1 %collective-permute-start.11 = (bf16[8,2,2048]{2,0,1:T(8,128)(2,1)S(1)}, bf16[8,2,2048]{2,0,1:T(8,128)(2,1)S(1)}, u32[]{:S(2)}, u32[]{:S(2)}) collective-permute-start(bf16[8,2,2048]{2,0,1:T(8,128)(2,1)S(1)} %copy.49), channel_id=1, source_target_pairs={{0,12},{1,13},{2,14},{3,15},{4,8},{5,9},{6,10},{7,11},{8,4},{9,5},... | collective-permute-start | bytes 196616 | tf_op jit(solution)/shard_map/ppermute | solution.py:22
  23.0 14.4 %collective-permute-start.12 = (bf16[8,2,2048]{2,0,1:T(8,128)(2,1)S(1)}, bf16[8,2,2048]{2,0,1:T(8,128)(2,1)S(1)}, u32[]{:S(2)}, u32[]{:S(2)}) collective-permute-start(bf16[8,2,2048]{2,0,1:T(8,128)(2,1)S(1)} %copy.50), channel_id=1, source_target_pairs={{0,13},{1,12},{2,15},{3,14},{4,9},{5,8},{6,11},{7,10},{8,5},{9,4},... | collective-permute-start | bytes 196616 | tf_op jit(solution)/shard_map/ppermute | solution.py:22
  27.4 13.1 %collective-permute-start.13 = (bf16[8,2,2048]{2,0,1:T(8,128)(2,1)S(1)}, bf16[8,2,2048]{2,0,1:T(8,128)(2,1)S(1)}, u32[]{:S(2)}, u32[]{:S(2)}) collective-permute-start(bf16[8,2,2048]{2,0,1:T(8,128)(2,1)S(1)} %copy.51), channel_id=1, source_target_pairs={{0,14},{1,15},{2,12},{3,13},{4,10},{5,11},{6,8},{7,9},{8,6},{9,7},... | collective-permute-start | bytes 196616 | tf_op jit(solution)/shard_map/ppermute | solution.py:22
  29.0 12.9 %collective-permute-start.14 = (bf16[8,2,2048]{2,0,1:T(8,128)(2,1)S(1)}, bf16[8,2,2048]{2,0,1:T(8,128)(2,1)S(1)}, u32[]{:S(2)}, u32[]{:S(2)}) collective-permute-start(bf16[8,2,2048]{2,0,1:T(8,128)(2,1)S(1)} %copy.52), channel_id=1, source_target_pairs={{0,15},{1,14},{2,13},{3,12},{4,11},{5,10},{6,9},{7,8},{8,7},{9,6},... | collective-permute-start | bytes 196616 | tf_op jit(solution)/shard_map/ppermute | solution.py:22
